TPU v7x, 32 devices: a whole 2x2x4 slice. The times are simulated.
32 devices in a mesh: pb: 8 (over z, y), ka: 4 (over x, core).
Axes of the slice: x: 2, y: 2, z: 4, core: 2. Of those that a mesh axis runs over, the one named last changes fastest.
Arguments:
- pair_trunk: bfloat16 [384, 384, 128], P('pb', 'ka'), may hold values from -40 to 40
- token_ids: int32 [3, 384], replicated, may hold values from 0 to 422, as said below
- w_rel: bfloat16 [139, 128], replicated, may hold values from -3.5 to 3.5
- cat_gain: float32 [256], replicated, may hold values from 0.1 to 1.9
- w_in: bfloat16 [256, 128], replicated, may hold values from -0.375 to 0.375
- trans_gain: float32 [2, 128], replicated, may hold values from 0.1 to 1.9
- trans_ab: bfloat16 [2, 128, 512], replicated, may hold values from -0.5 to 0.5
- trans_out: bfloat16 [2, 256, 128], replicated, may hold values from -0.375 to 0.375
- bias_gain: float32 [128], replicated, may hold values from 0.1 to 1.9
- w_bias: bfloat16 [128, 16], replicated, may hold values from -1.5 to 1.5
- normed: bfloat16 [8, 384, 768], P(None, 'pb', 'ka'), may hold values from -12 to 12
- w_proj: bfloat16 [4, 768, 768], P(None, None, 'ka'), may hold values from -1 to 1
- output_weight: bfloat16 [768, 768], P('ka'), may hold values from -0.21875 to 0.21875
Outputs:
- pair_cond: bfloat16 [384, 384, 128], P('pb', 'ka')
- update: bfloat16 [8, 384, 768], P(None, 'pb', 'ka')
Inputs may be any that keep to these rules, and one draw needn't show every extreme that they name: `token_ids`: row 0 is a token's residue number, row 1 its chain number, row 2 its entity number. Chain numbers start at 0 and never fall along the tokens; residue numbers never fall within a chain; all tokens of a chain share one entity. The last token's residue number is 422.
All inputs are finite; a program needn't handle non-finite values.
Results may differ from a plain program's by a relative error of at most 0.015.
The roundings to bfloat16 on the way count: a program that leaves them out, or rounds other values in their place, can miss the bound.
Values may be sent and summed in bfloat16 or wider, within the bound.
A program may use at most 64 MiB of HBM per device.

v0:
```python
import math
import jax
import jax.numpy as jnp
from jax import lax
from jax.sharding import PartitionSpec as P

HD = 48
RMAX = 32
SMAX = 2
REL = 139
EPS = 1e-05


def layer_norm(values, scaling):
    average = jnp.mean(values, axis=-1, keepdims=True)
    centered = values - average
    spread = jnp.mean(centered * centered, axis=-1, keepdims=True)
    return centered * lax.rsqrt(spread + EPS) * scaling


def relative_onehot(query_token_ids, key_ids, query_pos, key_pos):
    query_res = query_token_ids[0][:, None]
    key_res = key_ids[0][None, :]
    query_chain = query_token_ids[1][:, None]
    key_chain = key_ids[1][None, :]
    query_entity = query_token_ids[2][:, None]
    key_ent = key_ids[2][None, :]
    same_chain = query_chain == key_chain
    same_res = same_chain & (query_res == key_res)
    same_entity = query_entity == key_ent
    res_bins = 2 * RMAX + 2
    res_bin = jnp.where(same_chain, jnp.clip(query_res - key_res + RMAX, 0, 2 * RMAX), 2 * RMAX + 1)
    token_offset_bin = jnp.where(
        same_res, jnp.clip(query_pos[:, None] - key_pos[None, :] + RMAX, 0, 2 * RMAX), 2 * RMAX + 1
    )
    chain_offset_bin = jnp.where(
        same_entity, jnp.clip(query_chain - key_chain + SMAX, 0, 2 * SMAX), 2 * SMAX + 1
    )
    columns = jnp.arange(REL, dtype=jnp.int32)
    onehot = (columns == res_bin[..., None]) | (columns == (res_bins + token_offset_bin)[..., None])
    onehot = onehot | (columns == (2 * res_bins + chain_offset_bin)[..., None])
    onehot = onehot | (columns == REL - 1) & same_entity[..., None]
    return onehot.astype(jnp.bfloat16)


def condition_block(
    trunk_blk, onehot, w_rel, cat_gain, w_in, trans_gain, trans_ab, trans_out, bias_gain, w_bias
):
    half = trans_out.shape[1]
    relative = jnp.einsum("rkf,fc->rkc", onehot, w_rel, preferred_element_type=jnp.float32)
    joined = jnp.concatenate([trunk_blk.astype(jnp.float32), relative], axis=-1)
    normal_in = layer_norm(joined, cat_gain).astype(jnp.bfloat16)
    pair_state = jnp.einsum("rkf,fc->rkc", normal_in, w_in, preferred_element_type=jnp.float32)
    for layer_idx in range(2):
        normal_tr = layer_norm(pair_state, trans_gain[layer_idx]).astype(jnp.bfloat16)
        gate_up = jnp.einsum(
            "rkc,cf->rkf", normal_tr, trans_ab[layer_idx], preferred_element_type=jnp.float32
        )
        hidden = (jax.nn.silu(gate_up[..., :half]) * gate_up[..., half:]).astype(jnp.bfloat16)
        pair_state = pair_state + jnp.einsum(
            "rkf,fc->rkc", hidden, trans_out[layer_idx], preferred_element_type=jnp.float32
        )
    normal_b = layer_norm(pair_state, bias_gain).astype(jnp.bfloat16)
    bias_blk = jnp.einsum(
        "rkc,ch->hrk", normal_b, w_bias, preferred_element_type=jnp.float32
    ).astype(jnp.bfloat16)
    return (pair_state.astype(jnp.bfloat16), bias_blk)


def soft_weights(logits):
    row_max = jnp.max(logits, axis=-1, keepdims=True)
    expweights = jnp.exp(logits - row_max)
    return (expweights / jnp.sum(expweights, axis=-1, keepdims=True)).astype(jnp.bfloat16)


def shards(
    pair_trunk,
    token_ids,
    w_rel,
    cat_gain,
    w_in,
    trans_gain,
    trans_ab,
    trans_out,
    bias_gain,
    w_bias,
    normed,
    w_proj,
    output_weight,
):
    q_rows = pair_trunk.shape[0]
    k_rows = pair_trunk.shape[1]
    q_start = lax.axis_index("pb") * q_rows
    k_start = lax.axis_index("ka") * k_rows
    key_ids = lax.dynamic_slice_in_dim(token_ids, k_start, k_rows, 1)
    key_pos = k_start + jnp.arange(k_rows, dtype=jnp.int32)
    row_blk = 8

    def one_block(block_idx):
        begin_at = block_idx * row_blk
        trunk_blk = lax.dynamic_slice_in_dim(pair_trunk, begin_at, row_blk, 0)
        query_token_ids = lax.dynamic_slice_in_dim(token_ids, q_start + begin_at, row_blk, 1)
        query_pos = q_start + begin_at + jnp.arange(row_blk, dtype=jnp.int32)
        onehot = relative_onehot(query_token_ids, key_ids, query_pos, key_pos)
        return condition_block(
            trunk_blk,
            onehot,
            w_rel,
            cat_gain,
            w_in,
            trans_gain,
            trans_ab,
            trans_out,
            bias_gain,
            w_bias,
        )

    pair_blocks, bias_blocks = lax.map(one_block, jnp.arange(q_rows // row_blk, dtype=jnp.int32))
    pair_cond = pair_blocks.reshape(q_rows, k_rows, pair_blocks.shape[-1])
    bias_tile = jnp.transpose(bias_blocks, (1, 0, 2, 3)).reshape(
        bias_blocks.shape[1], q_rows, k_rows
    )
    samples = normed.shape[0]
    feat_local = normed.shape[2]
    heads_local = feat_local // HD
    scale_factor = 1.0 / math.sqrt(HD)
    projected = jnp.einsum(
        "sqf,pfe->psqe",
        lax.all_gather(normed, "ka", axis=2, tiled=True),
        w_proj,
        preferred_element_type=jnp.float32,
    )
    queries = projected[0].astype(jnp.bfloat16).reshape(samples, q_rows, heads_local, HD)
    kv_local = jnp.transpose(
        jnp.stack([projected[1], projected[2]], axis=1).astype(jnp.bfloat16), (0, 1, 3, 2)
    )
    bias_rows = lax.all_to_all(bias_tile, "ka", split_axis=0, concat_axis=2, tiled=True)
    kv_all = lax.all_gather(kv_local, "pb", axis=3, tiled=True)
    keys_all = kv_all[:, 0].reshape(samples, heads_local, HD, kv_all.shape[3])
    values_all = kv_all[:, 1].reshape(samples, heads_local, HD, kv_all.shape[3])
    logits = (
        jnp.einsum("sqhd,shdk->shqk", queries, keys_all, preferred_element_type=jnp.float32)
        * scale_factor
    )
    logits = logits + bias_rows[None].astype(jnp.float32)
    weights = soft_weights(logits)
    attended = jnp.einsum(
        "shqk,shdk->sqhd", weights, values_all, preferred_element_type=jnp.float32
    )
    gated_result = (
        attended.reshape(samples, q_rows, feat_local) * jax.nn.sigmoid(projected[3])
    ).astype(jnp.bfloat16)
    flat_gated = gated_result.reshape(samples * q_rows, feat_local)
    summed = lax.psum_scatter(
        jnp.einsum(
            "fe,nf->en", output_weight, flat_gated, preferred_element_type=jnp.float32
        ).astype(jnp.bfloat16),
        "ka",
        scatter_dimension=0,
        tiled=True,
    ).astype(jnp.float32)
    update = jnp.transpose(summed).reshape(samples, q_rows, feat_local).astype(jnp.bfloat16)
    return (pair_cond, update)


def solution(mesh):
    in_specs = (
        P("pb", "ka", None),
        P(),
        P(),
        P(),
        P(),
        P(),
        P(),
        P(),
        P(),
        P(),
        P(None, "pb", "ka"),
        P(None, None, "ka"),
        P("ka", None),
    )
    out_specs = (P("pb", "ka", None), P(None, "pb", "ka"))
    return jax.shard_map(shards, mesh=mesh, in_specs=in_specs, out_specs=out_specs, check_vma=False)
```

profile of v0, /device:TPU:0, one launch (start us, length us, event | category | flops | bytes accessed | tf_op | source)
XLA Modules:
  0.0 148.7 jit_solution(9345763957200801556)
XLA Ops:
  7.2 1.3 copy.25
  8.5 14.3 %all_gather.6 = bf16[8,48,768]{1,0,2:T(8,128)(2,1)S(1)} all-gather(bf16[8,48,192]{1,0,2:T(8,128)(2,1)S(1)} %copy.25), channel_id=1, replica_groups=mesh['pb'=8,'ka'=4] {'ka'}, dimensions={2}, use_global_device_ids=true | all-gather | bytes 737280 | tf_op jit(solution)/shard_map/all_gather | solution.py:129
  22.8 1.6 %copy.26 = bf16[8,48,768]{2,1,0:T(8,128)(2,1)} copy(bf16[8,48,768]{1,0,2:T(8,128)(2,1)S(1)} %all_gather.6) | data formatting | bytes 1179648 | tf_op jit(solution)/shard_map/all_gather | solution.py:129
  24.5 1.8 %fusion.70 = (bf16[4,8,48,192]{3,2,1,0:T(8,128)(2,1)S(1)}, f32[4,8,48,192]{3,2,1,0:T(8,128)S(1)}) fusion(bf16[8,48,768]{2,1,0:T(8,128)(2,1)} %copy.26, bf16[4,768,192]{1,2,0:T(8,128)(2,1)S(1)} %copy-done), kind=kOutput, calls=%fused_computation.118 | convolution fusion | flops 453279744 | bytes 3538944 | tf_op jit(solution)/shard_map/sqf,pfe->psqe/dot_general | solution.py:127
  28.2 60.4 %while.13 = (s32[]{:T(128)}, bf16[6,8,96,128]{3,2,1,0:T(8,128)(2,1)}, bf16[6,16,8,96]{3,1,2,0:T(8,128)(2,1)}, s32[6]{0:T(128)S(1)}, bf16[48,96,128]{2,1,0:T(8,12...) while((s32[]{:T(128)}, ...), condition=%wide.region_10.11_spmd.clone, body=%wide.region_0.10_spmd.clone.sunk | while | flops 390749440 | bytes 15165903 | solution.py:118
  31.4 1.1 fusion.91
  35.6 1.0 bitcast_dynamic-update-slice_fusion.2
  41.5 1.1 fusion.91
  51.6 1.1 fusion.91
  61.6 1.1 fusion.91
  71.7 1.1 fusion.91
  81.8 1.1 fusion.91
  85.9 1.0 bitcast_dynamic-update-slice_fusion.2
  88.6 1.7 %copy.48 = bf16[16,6,8,96]{3,2,1,0:T(8,128)(2,1)} copy(bf16[16,6,8,96]{3,0,2,1:T(8,128)(2,1)} %bitcast.136) | data formatting | bytes 294912 | tf_op jit(solution)/shard_map/transpose | solution.py:120
  90.3 4.0 %all-to-all-start = ((bf16[16,48,96]{2,1,0:T(8,128)(2,1)}), bf16[16,48,96]{2,1,0:T(8,128)(2,1)}, u32[]{:S(2)}, u32[]{:S(2)}) async-start(bf16[16,48,96]{2,1,0:T(8,128)(2,1)} %bitcast.106), calls=%async_computation | async-start | bytes 393216 | tf_op jit(solution)/shard_map/all_to_all | solution.py:137
  96.3 3.3 %all-to-all-done = bf16[16,48,96]{2,1,0:T(8,128)(2,1)} async-done(((bf16[16,48,96]{2,1,0:T(8,128)(2,1)}), bf16[16,48,96]{2,1,0:T(8,128)(2,1)}, u32[]{:S(2)}, u32[]{:S(2)}) %all-to-all-start) | async-done | bytes 147488 | tf_op jit(solution)/shard_map/all_to_all | solution.py:137
  101.8 3.4 %fusion.68 = (bf16[8,1,192,384]{2,3,0,1:T(8,128)(2,1)S(1)}, bf16[8,1,192,384]{2,3,0,1:T(8,128)(2,1)}) fusion(bf16[8,2,192,384]{2,3,0,1:T(8,128)(2,1)} %all-gather.2.cloned.1.call-done), kind=kLoop, calls=%fused_computation.116 | loop fusion | bytes 4718592 | tf_op jit(solution)/shard_map/slice | solution.py:139
  105.1 2.5 %copy.27 = bf16[8,1,192,384]{3,2,0,1:T(8,128)(2,1)} copy(bf16[8,1,192,384]{2,3,0,1:T(8,128)(2,1)} %get-tuple-element.183) | data formatting | bytes 2359296 | tf_op jit(solution)/shard_map/slice | solution.py:140
  107.7 1.5 %copy.28 = bf16[8,1,192,384]{3,2,0,1:T(8,128)(2,1)} copy(bf16[8,1,192,384]{2,3,0,1:T(8,128)(2,1)S(1)} %get-tuple-element.182) | data formatting | bytes 2359296 | tf_op jit(solution)/shard_map/slice | solution.py:139
  109.2 3.6 %fusion.71 = (f32[8,4,48]{2,1,0:T(4,128)S(1)}, f32[8,4,48,384]{3,2,1,0:T(8,128)}) fusion(f32[4,48,384]{2,1,0:T(8,128)} %reshape.365, bf16[8,4,48,384]{3,2,1,0:T(8,128)(2,1)} %bitcast.135, bf16[8,48,4,48]{3,2,1,0:T(4,128)(2,1)S(1)} %copy-done.5), kind=kOutput, calls=%fused_computation.119 | convolution fusion | flops 58982784 | bytes 3987456 | tf_op jit(solution)/shard_map/sub | solution.py:72
  112.8 2.3 %convolution_bitcast_fusion.1 = f32[8,48,4,48]{1,3,2,0:T(8,128)S(1)} fusion(bf16[8,4,48,384]{3,2,1,0:T(8,128)(2,1)S(1)} %bitcast.134, f32[8,4,48,384]{3,2,1,0:T(8,128)} %get-tuple-element.190, f32[8,4,48]{2,1,0:T(4,128)S(1)} %get-tuple-element.189), kind=kOutput, calls=%fused_computation.93 | convolution fusion | flops 57802752 | bytes 3840000 | tf_op jit(solution)/shard_map/shqk,shdk->sqhd/dot_general | solution.py:147
  116.5 1.1 copy.35
  117.6 22.5 %reduce-scatter.4.cloned.1.call-done = bf16[192,384]{1,0:T(8,128)(2,1)} async-done(((bf16[768,384]{1,0:T(8,128)(2,1)}), bf16[192,384]{1,0:T(8,128)(2,1)}) %reduce-scatter.4.cloned.1.call-update) | async-done | bytes 147472
  140.1 1.7 %copy.36 = bf16[192,384]{0,1:T(8,128)(2,1)} copy(bf16[192,384]{1,0:T(8,128)(2,1)} %reduce-scatter.4.cloned.1.call-done) | data formatting | bytes 294912
  (244 shorter events, 54.6 us)
Async XLA Ops:
  7.2 17.3 %copy-start = (bf16[4,768,192]{1,2,0:T(8,128)(2,1)S(1)}, bf16[4,768,192]{1,2,0:T(8,128)(2,1)}, u32[]{:S(2)}) copy-start(bf16[4,768,192]{1,2,0:T(8,128)(2,1)} %param.26) | copy-start | bytes 3538948
  7.2 94.6 %all-gather.2.cloned.1.call-start = ((), (), s32[]{:S(2)}) async-start(), calls=%async_computation.2 | async-start | bytes 3538944 | tf_op jit(solution)/shard_map/all_gather | solution.py:138
  26.3 1.7 %copy-start.9 = (s32[3,384]{1,0:T(4,128)S(1)}, s32[3,384]{1,0:T(4,128)}, u32[]{:S(2)}) copy-start(s32[3,384]{1,0:T(4,128)} %param.16) | copy-start | bytes 13828
  26.3 1.8 %copy-start.1 = (bf16[2,128,512]{2,1,0:T(8,128)(2,1)S(1)}, bf16[2,128,512]{2,1,0:T(8,128)(2,1)}, u32[]{:S(2)}) copy-start(bf16[2,128,512]{2,1,0:T(8,128)(2,1)} %param.21) | copy-start | bytes 786436
  26.4 1.8 %copy-start.7 = (bf16[128,16]{0,1:T(8,128)(2,1)S(1)}, bf16[128,16]{0,1:T(8,128)(2,1)}, u32[]{:S(2)}) copy-start(bf16[128,16]{0,1:T(8,128)(2,1)} %param.24) | copy-start | bytes 12292
  26.4 1.8 %copy-start.8 = (f32[2,128]{1,0:T(2,128)S(1)}, f32[2,128]{1,0:T(2,128)}, u32[]{:S(2)}) copy-start(f32[2,128]{1,0:T(2,128)} %param.20) | copy-start | bytes 3076
  26.4 1.7 %copy-start.10 = (f32[128]{0:T(128)S(1)}, f32[128]{0:T(128)}, u32[]{:S(2)}) copy-start(f32[128]{0:T(128)} %param.23) | copy-start | bytes 1540
  26.4 1.7 %copy-start.12 = (bf16[256,128]{1,0:T(8,128)(2,1)S(1)}, bf16[256,128]{1,0:T(8,128)(2,1)}, u32[]{:S(2)}) copy-start(bf16[256,128]{1,0:T(8,128)(2,1)} %param.19) | copy-start | bytes 196612
  26.4 1.7 %copy-start.13 = (bf16[139,128]{1,0:T(8,128)(2,1)S(1)}, bf16[139,128]{1,0:T(8,128)(2,1)}, u32[]{:S(2)}) copy-start(bf16[139,128]{1,0:T(8,128)(2,1)} %param.17) | copy-start | bytes 106756
  26.4 1.7 %copy-start.14 = (f32[256]{0:T(256)S(1)}, f32[256]{0:T(256)}, u32[]{:S(2)}) copy-start(f32[256]{0:T(256)} %param.18) | copy-start | bytes 3076
  33.5 0.9 copy-start.11
  43.5 0.9 copy-start.11
  53.6 0.9 copy-start.11
  63.7 0.9 copy-start.11
  73.7 0.9 copy-start.11
  83.8 0.9 copy-start.11
  88.6 5.9 %copy-start.4 = (bf16[1,8,48,192]{3,2,1,0:T(8,128)(2,1)S(1)}, bf16[1,8,48,192]{3,2,1,0:T(8,128)(2,1)}, u32[]{:S(2)}) copy-start(bf16[1,8,48,192]{3,2,1,0:T(8,128)(2,1)} %get-tuple-element.184) | copy-start | bytes 442372
  90.3 9.4 %all-to-all-start = ((bf16[16,48,96]{2,1,0:T(8,128)(2,1)}), bf16[16,48,96]{2,1,0:T(8,128)(2,1)}, u32[]{:S(2)}, u32[]{:S(2)}) async-start(bf16[16,48,96]{2,1,0:T(8,128)(2,1)} %bitcast.106), calls=%async_computation | async-start | bytes 393216 | tf_op jit(solution)/shard_map/all_to_all | solution.py:137
  94.3 45.9 %reduce-scatter.4.cloned.1.call-start = ((), (), s32[]{:S(2)}) async-start(), calls=%async_computation.3 | async-start | bytes 737280
  107.7 1.5 %copy-start.5 = (bf16[8,48,4,48]{3,2,1,0:T(4,128)(2,1)S(1)}, bf16[8,48,4,48]{3,2,1,0:T(4,128)(2,1)}, u32[]{:S(2)}) copy-start(bf16[8,48,4,48]{3,2,1,0:T(4,128)(2,1)} %convert_element_type.75) | copy-start | bytes 442372
  109.2 3.7 %copy-start.2 = (bf16[8,1,192,384]{3,2,0,1:T(8,128)(2,1)S(1)}, bf16[8,1,192,384]{3,2,0,1:T(8,128)(2,1)}, u32[]{:S(2)}) copy-start(bf16[8,1,192,384]{3,2,0,1:T(8,128)(2,1)} %copy.27) | copy-start | bytes 3538948
  115.1 1.0 copy-start.3
  115.1 1.1 copy-start.6
Sparse Core Ops, SparseCore 0:
  28.1 60.9 all-gather.1
  117.7 22.3 reduce-scatter.3
where the time goes:
time: 150 us; the launch traced here: 149 us
  matrix products  36 us (24%)
  waiting for transfers between devices  25.9 us (17%)
  other arithmetic  24.9 us (17%)
  local copies, waits for them, and re-layouts  24.6 us (16%)
  blocking collectives  14.3 us (10%)
  between operations  14.3 us (10%)
  loops' own time  4.55 us (3%)
  starting transfers between devices  4.06 us (3%)
    unnamed x3, waiting for transfers between devices  22.6 us
    all_gather x1, blocking collectives, shards(): lax.all_gather(normed, 'ka', axis=2, tiled=True)  14.3 us
    dot_general x12, matrix products, condition_block(): jnp.einsum('rkf,fc->rkc', hidden, trans_out[layer_idx], preferred_element...  8.85 us
    reduce_sum x24, other arithmetic, layer_norm(): spread = jnp.mean(centered * centered, axis=-1, keepdims=True)  8.37 us
    reduce_sum x12, other arithmetic, layer_norm(): average = jnp.mean(values, axis=-1, keepdims=True)  7.67 us
    dot_general x6, matrix products, condition_block(): jnp.einsum('rkc,ch->hrk', normal_b, w_bias, preferred_element_type=jnp.fl...  6.08 us
    convert_element_type x6, other arithmetic, condition_block(): joined = jnp.concatenate([trunk_blk.astype(jnp.float32), relative], axis=-1)  5.75 us
    dot_general x12, matrix products, condition_block(): jnp.einsum('rkc,cf->rkf', normal_tr, trans_ab[layer_idx], preferred_eleme...  5.08 us
  transfers between devices with their start and end apart: 3, of which 2 were waited for; matrix products, arithmetic and copies ran while one was open for 41% of the time, Pallas kernels for 0%

commit v1 on v0

--- a/solution.py
+++ b/solution.py
@@ -9,6 +9,17 @@
 SMAX = 2
 REL = 139
 EPS = 1e-05
+
+
+def gather_around(value, axis, dim):
+    ways = lax.axis_size(axis)
+    pieces = [value]
+    for far in range(1, ways):
+        pieces.append(
+            lax.ppermute(pieces[far - 1], axis, [(d, (d - 1) % ways) for d in range(ways)])
+        )
+    line = jnp.concatenate(pieces, axis=dim)
+    return jnp.roll(line, lax.axis_index(axis) * value.shape[dim], axis=dim)
 
 
 def layer_norm(values, scaling):
@@ -125,10 +136,7 @@
     heads_local = feat_local // HD
     scale_factor = 1.0 / math.sqrt(HD)
     projected = jnp.einsum(
-        "sqf,pfe->psqe",
-        lax.all_gather(normed, "ka", axis=2, tiled=True),
-        w_proj,
-        preferred_element_type=jnp.float32,
+        "sqf,pfe->psqe", gather_around(normed, "ka", 2), w_proj, preferred_element_type=jnp.float32
     )
     queries = projected[0].astype(jnp.bfloat16).reshape(samples, q_rows, heads_local, HD)
     kv_local = jnp.transpose(

time: 150 us -> 148 us (0.987)
  blocking collectives: 14.3 us -> 8.29 us
  waiting for transfers between devices: 25.9 us -> 31.7 us
  matrix products: 36 us -> 32.6 us
  starting transfers between devices: 4.06 us -> 6.24 us
    all_gather x1 -> x0, blocking collectives: 14.3 us -> none  [shards(): lax.all_gather(normed, 'ka', axis=2, tiled=True)]
    ppermute x0 -> x3, waiting for transfers between devices: none -> 9.12 us  [gather_around(): lax.ppermute(pieces[far - 1], axis, [(d, (d - 1) % ways) for d in range(w...]
    all_to_all x0 -> x1, blocking collectives: none -> 8.29 us  [shards(): lax.all_to_all(bias_tile, 'ka', split_axis=0, concat_axis=2, tiled=True)]
    ppermute x0 -> x3, starting transfers between devices: none -> 6.16 us  [gather_around(): lax.ppermute(pieces[far - 1], axis, [(d, (d - 1) % ways) for d in range(w...]
    dynamic_slice x6, local copies, waits for them, and re-layouts: 0.46 us -> 4.55 us  [one_block(): lax.dynamic_slice_in_dim(token_ids, q_start + begin_at, row_blk, 1)]
    all_to_all x1 -> x0, starting transfers between devices: 3.99 us -> none  [shards(): lax.all_to_all(bias_tile, 'ka', split_axis=0, concat_axis=2, tiled=True)]
    dot_general x6, matrix products: 6.08 us -> 2.41 us  [condition_block(): jnp.einsum('rkc,ch->hrk', normal_b, w_bias, preferred_element_type=jnp.fl...]
    all_to_all x1 -> x0, waiting for transfers between devices: 3.34 us -> none  [shards(): lax.all_to_all(bias_tile, 'ka', split_axis=0, concat_axis=2, tiled=True)]
  transfers between devices with their start and end apart: 3 -> 5, of which waited for: 2 -> 4; matrix products, arithmetic and copies ran while one was open for 41% -> 40% of each run, Pallas kernels for 0% -> 0%
where the time goes in v1:
time: 148 us; the launch traced here: 147 us
  matrix products  32.6 us (22%)
  waiting for transfers between devices  31.7 us (21%)
  other arithmetic  25.1 us (17%)
  local copies, waits for them, and re-layouts  24.3 us (16%)
  between operations  14.3 us (10%)
  blocking collectives  8.29 us (6%)
  starting transfers between devices  6.24 us (4%)
  loops' own time  4.99 us (3%)
    unnamed x3, waiting for transfers between devices  22.6 us
    ppermute x3, waiting for transfers between devices, gather_around(): lax.ppermute(pieces[far - 1], axis, [(d, (d - 1) % ways) for d in range(w...  9.12 us
    dot_general x12, matrix products, condition_block(): jnp.einsum('rkf,fc->rkc', hidden, trans_out[layer_idx], preferred_element...  8.85 us
    reduce_sum x24, other arithmetic, layer_norm(): spread = jnp.mean(centered * centered, axis=-1, keepdims=True)  8.39 us
    all_to_all x1, blocking collectives, shards(): lax.all_to_all(bias_tile, 'ka', split_axis=0, concat_axis=2, tiled=True)  8.29 us
    reduce_sum x12, other arithmetic, layer_norm(): average = jnp.mean(values, axis=-1, keepdims=True)  7.64 us
    ppermute x3, starting transfers between devices, gather_around(): lax.ppermute(pieces[far - 1], axis, [(d, (d - 1) % ways) for d in range(w...  6.16 us
    slice x2, local copies, waits for them, and re-layouts, shards(): keys_all = kv_all[:, 0].reshape(samples, heads_local, HD, kv_all.shape[3])  5.78 us
  transfers between devices with their start and end apart: 5, of which 4 were waited for; matrix products, arithmetic and copies ran while one was open for 40% of the time, Pallas kernels for 0%

profile of v1, /device:TPU:0, one launch (start us, length us, event | category | flops | bytes accessed | tf_op | source)
XLA Modules:
  0.0 147.4 jit_solution(1195766167117176327)
XLA Ops:
  7.2 2.5 %collective-permute-start = (bf16[8,48,192]{2,1,0:T(8,128)(2,1)}, bf16[8,48,192]{2,1,0:T(8,128)(2,1)S(1)}, u32[]{:S(2)}, u32[]{:S(2)}) collective-permute-start(bf16[8,48,192]{2,1,0:T(8,128)(2,1)} %param.25), channel_id=1, source_target_pairs={{0,3},{1,0},{2,1},{3,2},{4,7},{5,4},{6,5},{7,6},{8,11},{9,8},{10,9... | collective-permute-start | bytes 442376 | tf_op jit(solution)/shard_map/ppermute | solution.py:19
  9.7 3.5 %collective-permute-done = bf16[8,48,192]{2,1,0:T(8,128)(2,1)S(1)} collective-permute-done((bf16[8,48,192]{2,1,0:T(8,128)(2,1)}, bf16[8,48,192]{2,1,0:T(8,128)(2,1)S(1)}, u32[]{:S(2)}, u32[]{:S(2)}) %collective-permute-start) | collective-permute-done | bytes 147488 | tf_op jit(solution)/shard_map/ppermute | solution.py:19
  13.2 1.8 %collective-permute-start.1 = (bf16[8,48,192]{2,1,0:T(8,128)(2,1)S(1)}, bf16[8,48,192]{2,1,0:T(8,128)(2,1)S(1)}, u32[]{:S(2)}, u32[]{:S(2)}) collective-permute-start(bf16[8,48,192]{2,1,0:T(8,128)(2,1)S(1)} %collective-permute-done), channel_id=1, source_target_pairs={{0,3},{1,0},{2,1},{3,2},{4,7},{5,4},{6,5},{7,6},{8,11},{9,8},{10,9... | collective-permute-start | bytes 442376 | tf_op jit(solution)/shard_map/ppermute | solution.py:19
  15.0 3.2 %collective-permute-done.1 = bf16[8,48,192]{2,1,0:T(8,128)(2,1)S(1)} collective-permute-done((bf16[8,48,192]{2,1,0:T(8,128)(2,1)S(1)}, bf16[8,48,192]{2,1,0:T(8,128)(2,1)S(1)}, u32[]{:S(2)}, u32[]{:S(2)}) %collective-permute-start.1) | collective-permute-done | bytes 147488 | tf_op jit(solution)/shard_map/ppermute | solution.py:19
  18.2 1.9 %collective-permute-start.2 = (bf16[8,48,192]{2,1,0:T(8,128)(2,1)S(1)}, bf16[8,48,192]{2,1,0:T(8,128)(2,1)S(1)}, u32[]{:S(2)}, u32[]{:S(2)}) collective-permute-start(bf16[8,48,192]{2,1,0:T(8,128)(2,1)S(1)} %collective-permute-done.1), channel_id=1, source_target_pairs={{0,3},{1,0},{2,1},{3,2},{4,7},{5,4},{6,5},{7,6},{8,11},{9,8},{10,9... | collective-permute-start | bytes 442376 | tf_op jit(solution)/shard_map/ppermute | solution.py:19
  20.8 2.4 %collective-permute-done.2 = bf16[8,48,192]{2,1,0:T(8,128)(2,1)S(1)} collective-permute-done((bf16[8,48,192]{2,1,0:T(8,128)(2,1)S(1)}, bf16[8,48,192]{2,1,0:T(8,128)(2,1)S(1)}, u32[]{:S(2)}, u32[]{:S(2)}) %collective-permute-start.2) | collective-permute-done | bytes 147488 | tf_op jit(solution)/shard_map/ppermute | solution.py:19
  23.3 2.2 %concatenate.9 = bf16[8,48,1536]{2,1,0:T(8,128)(2,1)S(1)} concatenate(bf16[8,48,192]{2,1,0:T(8,128)(2,1)} %param.25, bf16[8,48,192]{2,1,0:T(8,128)(2,1)S(1)} %collective-permute-done, bf16[8,48,192]{2,1,0:T(8,128)(2,1)S(1)} %collective-permute-done.1, bf16[8,48,192]{2,1,0:T(8,128)(2,1)S(1)} %collective-permute-done.2, bf16[8,48,192]{2,1,0:T(8,128)(2,1)} %param.25, ...), dimensions={2} | concatenate | bytes 2359296 | tf_op jit(solution)/shard_map/jit(_roll_dynamic)/concatenate | solution.py:22
  25.5 2.0 %fusion.72 = (bf16[4,8,48,192]{3,2,0,1:T(8,128)(2,1)S(1)}, f32[4,8,48,192]{3,2,0,1:T(8,128)}) fusion(bf16[4,768,192]{1,2,0:T(8,128)(2,1)S(1)} %copy-done, bf16[8,48,1536]{2,1,0:T(8,128)(2,1)S(1)} %concatenate.9, s32[]{:T(128)S(6)} %select_n.46), kind=kOutput, calls=%fused_computation.120 | convolution fusion | flops 453279744 | bytes 3538948 | tf_op jit(solution)/shard_map/sqf,pfe->psqe/dot_general | solution.py:138
  28.6 60.8 %while.13 = (s32[]{:T(128)}, bf16[6,8,96,128]{3,2,1,0:T(8,128)(2,1)}, bf16[6,16,8,96]{3,1,2,0:T(8,128)(2,1)S(1)}, s32[6]{0:T(128)S(1)}, bf16[48,96,128]{2,1,0:T(...) while((s32[]{:T(128)}, ...), condition=%wide.region_10.11_spmd.clone, body=%wide.region_0.10_spmd.clone.sunk | while | flops 390749440 | bytes 14643635 | solution.py:129
  30.9 1.1 fusion.93
  41.0 1.1 fusion.93
  51.1 1.1 fusion.93
  61.3 1.1 fusion.93
  71.4 1.1 fusion.93
  81.6 1.1 fusion.93
  89.5 8.3 %all_to_all.4 = bf16[16,48,96]{2,1,0:T(8,128)(2,1)S(1)} all-to-all(bf16[16,48,96]{2,1,0:T(8,128)(2,1)S(1)} %bitcast.140), channel_id=1, replica_groups=mesh['pb'=8,'ka'=4] {'ka'}, dimensions={0} | all-to-all | bytes 294912 | tf_op jit(solution)/shard_map/all_to_all | solution.py:145
  99.3 1.1 fusion.56
  100.6 3.3 %fusion.70 = (bf16[8,1,192,384]{2,3,0,1:T(8,128)(2,1)}, bf16[8,1,192,384]{2,3,0,1:T(8,128)(2,1)S(1)}) fusion(bf16[8,2,192,384]{2,3,0,1:T(8,128)(2,1)} %all-gather.2.cloned.1.call-done), kind=kLoop, calls=%fused_computation.118 | loop fusion | bytes 4718592 | tf_op jit(solution)/shard_map/slice | solution.py:147
  103.9 2.5 %copy.29 = bf16[8,1,192,384]{3,2,0,1:T(8,128)(2,1)} copy(bf16[8,1,192,384]{2,3,0,1:T(8,128)(2,1)} %get-tuple-element.182) | data formatting | bytes 2359296 | tf_op jit(solution)/shard_map/slice | solution.py:147
  106.4 1.5 %copy.28 = bf16[8,1,192,384]{3,2,0,1:T(8,128)(2,1)} copy(bf16[8,1,192,384]{2,3,0,1:T(8,128)(2,1)S(1)} %get-tuple-element.183) | data formatting | bytes 2359296 | tf_op jit(solution)/shard_map/slice | solution.py:148
  107.9 3.7 %fusion.73 = (f32[8,4,48]{2,1,0:T(4,128)S(1)}, f32[8,4,48,384]{3,2,1,0:T(8,128)}) fusion(f32[4,48,384]{2,1,0:T(8,128)S(1)} %reshape.365, bf16[8,4,48,384]{3,2,1,0:T(8,128)(2,1)} %bitcast.138, bf16[8,48,4,48]{3,2,1,0:T(4,128)(2,1)} %convert_element_type.75), kind=kOutput, calls=%fused_computation.121 | convolution fusion | flops 58982784 | bytes 3987456 | tf_op jit(solution)/shard_map/sub | solution.py:83
  111.6 2.3 %convolution_bitcast_fusion.1 = f32[8,48,4,48]{1,3,2,0:T(8,128)S(1)} fusion(bf16[8,4,48,384]{3,2,1,0:T(8,128)(2,1)S(1)} %bitcast.139, f32[8,4,48,384]{3,2,1,0:T(8,128)} %get-tuple-element.190, f32[8,4,48]{2,1,0:T(4,128)S(1)} %get-tuple-element.189), kind=kOutput, calls=%fused_computation.93 | convolution fusion | flops 57802752 | bytes 3840000 | tf_op jit(solution)/shard_map/shqk,shdk->sqhd/dot_general | solution.py:155
  116.3 22.5 %reduce-scatter.4.cloned.1.call-done = bf16[192,384]{1,0:T(8,128)(2,1)} async-done(((bf16[768,384]{1,0:T(8,128)(2,1)}), bf16[192,384]{1,0:T(8,128)(2,1)}) %reduce-scatter.4.cloned.1.call-update) | async-done | bytes 147472
  138.8 1.7 %copy.37 = bf16[192,384]{0,1:T(8,128)(2,1)} copy(bf16[192,384]{1,0:T(8,128)(2,1)} %reduce-scatter.4.cloned.1.call-done) | data formatting | bytes 294912
  (229 shorter events, 55.3 us)
Async XLA Ops:
  7.2 18.4 %copy-start = (bf16[4,768,192]{1,2,0:T(8,128)(2,1)S(1)}, bf16[4,768,192]{1,2,0:T(8,128)(2,1)}, u32[]{:S(2)}) copy-start(bf16[4,768,192]{1,2,0:T(8,128)(2,1)} %param.26) | copy-start | bytes 3538948
  7.2 93.4 %all-gather.2.cloned.1.call-start = ((), (), s32[]{:S(2)}) async-start(), calls=%async_computation.2 | async-start | bytes 3538944 | tf_op jit(solution)/shard_map/all_gather | solution.py:146
  7.2 6.0 %collective-permute-start = (bf16[8,48,192]{2,1,0:T(8,128)(2,1)}, bf16[8,48,192]{2,1,0:T(8,128)(2,1)S(1)}, u32[]{:S(2)}, u32[]{:S(2)}) collective-permute-start(bf16[8,48,192]{2,1,0:T(8,128)(2,1)} %param.25), channel_id=1, source_target_pairs={{0,3},{1,0},{2,1},{3,2},{4,7},{5,4},{6,5},{7,6},{8,11},{9,8},{10,9... | collective-permute-start | bytes 442376 | tf_op jit(solution)/shard_map/ppermute | solution.py:19
  13.2 5.0 %collective-permute-start.1 = (bf16[8,48,192]{2,1,0:T(8,128)(2,1)S(1)}, bf16[8,48,192]{2,1,0:T(8,128)(2,1)S(1)}, u32[]{:S(2)}, u32[]{:S(2)}) collective-permute-start(bf16[8,48,192]{2,1,0:T(8,128)(2,1)S(1)} %collective-permute-done), channel_id=1, source_target_pairs={{0,3},{1,0},{2,1},{3,2},{4,7},{5,4},{6,5},{7,6},{8,11},{9,8},{10,9... | collective-permute-start | bytes 442376 | tf_op jit(solution)/shard_map/ppermute | solution.py:19
  18.2 5.1 %collective-permute-start.2 = (bf16[8,48,192]{2,1,0:T(8,128)(2,1)S(1)}, bf16[8,48,192]{2,1,0:T(8,128)(2,1)S(1)}, u32[]{:S(2)}, u32[]{:S(2)}) collective-permute-start(bf16[8,48,192]{2,1,0:T(8,128)(2,1)S(1)} %collective-permute-done.1), channel_id=1, source_target_pairs={{0,3},{1,0},{2,1},{3,2},{4,7},{5,4},{6,5},{7,6},{8,11},{9,8},{10,9... | collective-permute-start | bytes 442376 | tf_op jit(solution)/shard_map/ppermute | solution.py:19
  27.5 1.0 copy-start.1
  27.5 1.0 copy-start.4
  27.5 1.0 copy-start.5
  27.5 1.1 copy-start.6
  27.5 1.1 copy-start.7
  27.5 1.1 copy-start.8
  27.5 1.1 copy-start.9
  27.6 1.1 copy-start.10
  28.5 110.4 %reduce-scatter.4.cloned.1.call-start = ((), (), s32[]{:S(2)}) async-start(), calls=%async_computation.3 | async-start | bytes 737280
  107.9 3.7 %copy-start.2 = (bf16[8,1,192,384]{3,2,0,1:T(8,128)(2,1)S(1)}, bf16[8,1,192,384]{3,2,0,1:T(8,128)(2,1)}, u32[]{:S(2)}) copy-start(bf16[8,1,192,384]{3,2,0,1:T(8,128)(2,1)} %copy.28) | copy-start | bytes 3538948
  113.9 1.0 copy-start.3
Sparse Core Ops, SparseCore 0:
  28.6 61.6 all-gather.1
  116.4 22.3 reduce-scatter.3
